TPU v7x, 32 devices: a whole 2x2x4 slice. The times are simulated.
32 devices in a mesh: seq: 8 (over z, y), feat: 4 (over x, core).
Axes of the slice: x: 2, y: 2, z: 4, core: 2. Of those that a mesh axis runs over, the one named last changes fastest.
Arguments:
- activations_in: bfloat16 [6144, 512], P('seq', 'feat'), may hold values from -6 to 6
- cotangent: bfloat16 [6144, 512], P('seq', 'feat'), may hold values from -6 to 6
- seq_start: int32 [16], P('seq'), may hold values from 0 to 768, as said below
- seq_length: int32 [16], P('seq'), may hold values from 0 to 768, as said below
- input_matrix: float32 [2, 512, 768], P(None, 'feat'), may hold values from -0.25 to 0.25
- output_matrix: float32 [2, 1536, 512], P(None, None, 'feat'), may hold values from -1.25 to 1.25
- gate_matrix: float32 [2, 512, 512], P(None, None, 'feat'), may hold values from -0.25 to 0.25
- feature_vectors: float32 [2, 4, 512], P(None, None, 'feat'), may hold values from 0.1 to 1.9
- state_vectors: float32 [2, 3, 384], replicated, may hold values from -20 to 20, as said below
- velocity_input: float32 [2, 512, 768], P(None, 'feat'), may hold values from -6 to 6
- velocity_output: float32 [2, 1536, 512], P(None, None, 'feat'), may hold values from -6 to 6
- velocity_gate: float32 [2, 512, 512], P(None, None, 'feat'), may hold values from -6 to 6
- velocity_feature: float32 [2, 4, 512], P(None, None, 'feat'), may hold values from -6 to 6
- velocity_state: float32 [2, 3, 384], replicated, may hold values from -6 to 6
- average_input: float32 [2, 512, 768], P(None, 'feat'), may hold values from -0.25 to 0.25
- average_output: float32 [2, 1536, 512], P(None, None, 'feat'), may hold values from -1.25 to 1.25
- average_gate: float32 [2, 512, 512], P(None, None, 'feat'), may hold values from -0.25 to 0.25
- average_feature: float32 [2, 4, 512], P(None, None, 'feat'), may hold values from 0.1 to 1.9
- average_state: float32 [2, 3, 384], replicated, may hold values from -3 to 1
Outputs:
- activations_out: float32 [6144, 512], P('seq', 'feat')
- input_gradient: float32 [6144, 512], P('seq', 'feat')
- gradient_input: float32 [2, 512, 768], P(None, 'feat')
- gradient_output: float32 [2, 1536, 512], P(None, None, 'feat')
- gradient_gate: float32 [2, 512, 512], P(None, None, 'feat')
- gradient_feature: float32 [2, 4, 512], P(None, None, 'feat')
- gradient_state: float32 [2, 3, 384], replicated
- updated_input: float32 [2, 512, 768], P(None, 'feat')
- updated_output: float32 [2, 1536, 512], P(None, None, 'feat')
- updated_gate: float32 [2, 512, 512], P(None, None, 'feat')
- updated_feature: float32 [2, 4, 512], P(None, None, 'feat')
- state_change: float32 [2, 3, 384], replicated
- momentum_input: float32 [2, 512, 768], P(None, 'feat')
- momentum_output: float32 [2, 1536, 512], P(None, None, 'feat')
- momentum_gate: float32 [2, 512, 512], P(None, None, 'feat')
- momentum_feature: float32 [2, 4, 512], P(None, None, 'feat')
- momentum_state: float32 [2, 3, 384], replicated
- smoothed_input: float32 [2, 512, 768], P(None, 'feat')
- smoothed_output: float32 [2, 1536, 512], P(None, None, 'feat')
- smoothed_gate: float32 [2, 512, 512], P(None, None, 'feat')
- smoothed_feature: float32 [2, 4, 512], P(None, None, 'feat')
- smoothed_state: float32 [2, 3, 384], replicated
Inputs may be any that keep to these rules, and one draw needn't show every extreme that they name: `seq_length`: sequences of a device lie in its own buffer, ordered and without intersection; one device holds a single sequence of 768 tokens and an empty slot, every other device two sequences of 192 to 384 tokens. `seq_start`: positions within a device's buffer; a slot of length zero starts at 768. `state_vectors`: rows hold log(-Re Lambda), Im Lambda and the log timestep.
All inputs are finite; a program needn't handle non-finite values.
Results may differ from a plain program's by a relative error of at most 0.012.
The roundings to bfloat16 on the way count: a program that leaves them out, or rounds other values in their place, can miss the bound.
Values may be sent and summed in bfloat16 or wider, within the bound.
A program may use at most 448 MiB of HBM per device.

v0:
```python
import math
import jax
import jax.numpy as jnp
from jax import lax
from jax.sharding import PartitionSpec as P

epsilon = 1e-05
momentum = 0.9
smoothing = 0.5
slow_rate = 0.02
main_rate = 0.05
weight_decay = 0.1


def smooth(value):
    return jax.nn.gelu(value, approximate=False)


def combine(earlier, later):
    mult_real = later[0] * earlier[0] - later[1] * earlier[1]
    mult_imag = later[0] * earlier[1] + later[1] * earlier[0]
    add_real = later[0] * earlier[2] - later[1] * earlier[3] + later[2]
    add_imag = later[0] * earlier[3] + later[1] * earlier[2] + later[3]
    return (mult_real, mult_imag, add_real, add_imag)


def masks_of(starts, lengths, count):
    position = jnp.arange(count, dtype=jnp.int32)[:, None]
    begin = starts[None, :]
    finish = begin + lengths[None, :]
    inside = (position >= begin) & (position < finish)
    alive = jnp.any(inside, 1)
    opening = jnp.any(inside & (position == begin), 1)
    closing = jnp.any(inside & (position == finish - 1), 1)
    return (
        alive.astype(jnp.float32),
        (alive & ~opening).astype(jnp.float32),
        (alive & ~closing).astype(jnp.float32),
    )


def prefix(current, backward):
    length = current[2].shape[0]
    offset = 1
    while offset < length:

        def shifted(value):
            filler = jnp.zeros((offset,) + value.shape[1:], value.dtype)
            if backward:
                return jnp.concatenate([value[offset:], filler], 0)
            return jnp.concatenate([filler, value[: length - offset]], 0)

        earlier = tuple((shifted(value) for value in current))
        current = combine(earlier, current)
        offset = offset * 2
    return current


def scan_states(drive, state_row, alive, carry_prev, carry_next):
    width = state_row.shape[1]
    rate = -jnp.exp(state_row[0])
    frequency = state_row[1]
    timestep = jnp.exp(state_row[2])
    decay = jnp.exp(rate * timestep)
    angle = frequency * timestep
    pole_real = decay * jnp.cos(angle)
    pole_imag = decay * jnp.sin(angle)
    denom = rate * rate + frequency * frequency
    factor_real = ((pole_real - 1.0) * rate + pole_imag * frequency) / denom
    factor_imag = (pole_imag * rate - (pole_real - 1.0) * frequency) / denom
    drive_real = drive[:, :width]
    drive_imag = drive[:, width:]
    input_real = (drive_real * factor_real - drive_imag * factor_imag) * alive[:, None]
    input_imag = (drive_real * factor_imag + drive_imag * factor_real) * alive[:, None]
    ahead = prefix(
        (carry_prev[:, None] * pole_real, carry_prev[:, None] * pole_imag, input_real, input_imag),
        False,
    )
    behind = prefix(
        (carry_next[:, None] * pole_real, carry_next[:, None] * pole_imag, input_real, input_imag),
        True,
    )
    return jnp.concatenate([ahead[2], ahead[3], behind[2], behind[3]], 1)


def update(weight, gradient, velocity, average, rate, decay):
    adjusted = gradient + decay * weight
    velocity_new = momentum * velocity + adjusted
    change = -rate * (adjusted + momentum * velocity_new)
    weight_new = weight + change
    average_new = smoothing * average + (1.0 - smoothing) * weight_new
    return (weight_new, velocity_new, average_new, change)


def contract_rows(left, right):
    return lax.dot_general(
        left, right, (((0,), (0,)), ((), ())), preferred_element_type=jnp.float32
    )


def contract_cols(left, right):
    return lax.dot_general(
        left, right, (((1,), (1,)), ((), ())), preferred_element_type=jnp.float32
    )


def moments(stream):
    whole = lax.all_gather(stream, "feat", axis=1, tiled=True)
    center = jnp.mean(whole, 1, keepdims=True)
    spread = whole - center
    variance = jnp.mean(spread * spread, 1, keepdims=True)
    return (center, lax.rsqrt(variance + epsilon))


def back_moments(unit_grad, unit):
    spread_grad, crossed = (
        lax.all_gather(unit_grad, "feat", axis=1, tiled=True),
        lax.all_gather(unit_grad * unit, "feat", axis=1, tiled=True),
    )
    return (jnp.mean(spread_grad, 1, keepdims=True), jnp.mean(crossed, 1, keepdims=True))


def state_forward(normed_low, in_low, state_row, masks):
    partial_drive = jnp.dot(normed_low, in_low, preferred_element_type=jnp.float32)
    drive = lax.psum(partial_drive, "feat")
    states = scan_states(drive, state_row, masks[0], masks[1], masks[2])
    return (drive, states.astype(jnp.bfloat16))


def state_backward(drive, state_row, masks, mixed_low, out_low):

    def scanned(drive_in, rows_in):
        return scan_states(drive_in, rows_in, masks[0], masks[1], masks[2])

    partial_states = contract_cols(mixed_low, out_low)
    states_grad = lax.psum(partial_states, "feat")
    unused, pull = jax.vjp(scanned, drive, state_row)
    drive_grad, row_grad = pull(states_grad)
    return (drive_grad.astype(jnp.bfloat16), row_grad)


def body(
    activations_in,
    cotangent,
    seq_start,
    seq_length,
    input_matrix,
    output_matrix,
    gate_matrix,
    feature_vectors,
    state_vectors,
    velocity_input,
    velocity_output,
    velocity_gate,
    velocity_feature,
    velocity_state,
    average_input,
    average_output,
    average_gate,
    average_feature,
    average_state,
):
    count = activations_in.shape[0]
    layers = input_matrix.shape[0]
    masks = masks_of(seq_start, seq_length, count)
    stream = activations_in.astype(jnp.float32)
    saved = []
    for layer in range(layers):
        in_low = input_matrix[layer].astype(jnp.bfloat16)
        out_low = output_matrix[layer].astype(jnp.bfloat16)
        gate_low = gate_matrix[layer].astype(jnp.bfloat16)
        feature_row = feature_vectors[layer]
        center, scale = moments(stream)
        unit = (stream - center) * scale
        normed = unit * feature_row[0] + feature_row[1]
        normed_low = normed.astype(jnp.bfloat16)
        drive, states_low = state_forward(normed_low, in_low, state_vectors[layer], masks)
        mixed = (
            jnp.dot(states_low, out_low, preferred_element_type=jnp.float32)
            + feature_row[2] * normed
        )
        act = smooth(mixed)
        act_all = lax.all_gather(act.astype(jnp.bfloat16), "feat", axis=1, tiled=True)
        pre = jnp.dot(act_all, gate_low, preferred_element_type=jnp.float32) + feature_row[3]
        saved.append((scale, unit, normed, normed_low, drive, states_low, mixed, act, act_all, pre))
        stream = stream + act * jax.nn.sigmoid(pre)
    grad = cotangent.astype(jnp.float32) * masks[0][:, None]
    layer_grads = [None] * layers
    for layer in reversed(range(layers)):
        scale, unit, normed, normed_low, drive, states_low, mixed, act, act_all, pre = saved[layer]
        in_low = input_matrix[layer].astype(jnp.bfloat16)
        out_low = output_matrix[layer].astype(jnp.bfloat16)
        gate_low = gate_matrix[layer].astype(jnp.bfloat16)
        feature_row = feature_vectors[layer]
        gate = jax.nn.sigmoid(pre)
        pre_grad = (grad * act * gate * (1.0 - gate)).astype(jnp.bfloat16)
        gate_grad = contract_rows(act_all, pre_grad)
        gate_bias_grad = jnp.sum(pre_grad.astype(jnp.float32), 0)
        act_grad = grad * gate + lax.psum_scatter(
            contract_cols(pre_grad, gate_low), "feat", scatter_dimension=1, tiled=True
        )
        mixed_grad = jax.vjp(smooth, mixed)[1](act_grad)[0]
        skip_grad = jnp.sum(mixed_grad * normed, 0)
        mixed_low = mixed_grad.astype(jnp.bfloat16)
        out_grad = contract_rows(states_low, mixed_low)
        drive_low, row_grad = state_backward(drive, state_vectors[layer], masks, mixed_low, out_low)
        in_grad = contract_rows(normed_low, drive_low)
        normed_grad = mixed_grad * feature_row[2] + contract_cols(drive_low, in_low)
        gain_grad = jnp.sum(normed_grad * unit, 0)
        bias_grad = jnp.sum(normed_grad, 0)
        unit_grad = normed_grad * feature_row[0]
        first_mean, second_mean = back_moments(unit_grad, unit)
        grad = grad + scale * (unit_grad - first_mean - unit * second_mean)
        feature_grad = jnp.stack([gain_grad, bias_grad, skip_grad, gate_bias_grad])
        layer_grads[layer] = (in_grad, out_grad, gate_grad, feature_grad, row_grad)
    stacked_in = jnp.stack([entry[0] for entry in layer_grads])
    stacked_out = jnp.stack([entry[1] for entry in layer_grads])
    stacked_gate = jnp.stack([entry[2] for entry in layer_grads])
    stacked_feature = jnp.stack([entry[3] for entry in layer_grads])
    stacked_state = jnp.stack([entry[4] for entry in layer_grads])
    summed = lax.psum(
        (stacked_in, stacked_out, stacked_gate, stacked_feature, stacked_state), "seq"
    )
    factor = 1.0 / math.sqrt(count * lax.axis_size("seq"))
    grad_in = summed[0] * factor
    grad_out = summed[1] * factor
    grad_gate = summed[2] * factor
    grad_feature = summed[3] * factor
    grad_state = summed[4] * factor
    new_in = update(input_matrix, grad_in, velocity_input, average_input, slow_rate, 0.0)
    new_out = update(output_matrix, grad_out, velocity_output, average_output, slow_rate, 0.0)
    new_gate = update(gate_matrix, grad_gate, velocity_gate, average_gate, main_rate, weight_decay)
    new_feature = update(
        feature_vectors, grad_feature, velocity_feature, average_feature, main_rate, weight_decay
    )
    new_state = update(state_vectors, grad_state, velocity_state, average_state, slow_rate, 0.0)
    return (
        stream,
        grad,
        grad_in,
        grad_out,
        grad_gate,
        grad_feature,
        grad_state,
        new_in[0],
        new_out[0],
        new_gate[0],
        new_feature[0],
        new_state[3],
        new_in[1],
        new_out[1],
        new_gate[1],
        new_feature[1],
        new_state[1],
        new_in[2],
        new_out[2],
        new_gate[2],
        new_feature[2],
        new_state[2],
    )


def solution(mesh):
    return jax.shard_map(
        body,
        mesh=mesh,
        in_specs=(
            P("seq", "feat"),
            P("seq", "feat"),
            P("seq"),
            P("seq"),
            P(None, "feat", None),
            P(None, None, "feat"),
            P(None, None, "feat"),
            P(None, None, "feat"),
            P(),
            P(None, "feat", None),
            P(None, None, "feat"),
            P(None, None, "feat"),
            P(None, None, "feat"),
            P(),
            P(None, "feat", None),
            P(None, None, "feat"),
            P(None, None, "feat"),
            P(None, None, "feat"),
            P(),
        ),
        out_specs=(
            P("seq", "feat"),
            P("seq", "feat"),
            P(None, "feat", None),
            P(None, None, "feat"),
            P(None, None, "feat"),
            P(None, None, "feat"),
            P(),
            P(None, "feat", None),
            P(None, None, "feat"),
            P(None, None, "feat"),
            P(None, None, "feat"),
            P(),
            P(None, "feat", None),
            P(None, None, "feat"),
            P(None, None, "feat"),
            P(None, None, "feat"),
            P(),
            P(None, "feat", None),
            P(None, None, "feat"),
            P(None, None, "feat"),
            P(None, None, "feat"),
            P(),
        ),
        check_vma=False,
    )
```

profile of v0, /device:TPU:0, one launch (start us, length us, event | category | flops | bytes accessed | tf_op | source)
XLA Modules:
  0.0 1222.3 jit_solution(16966885579422786372)
XLA Ops:
  10.5 22.2 %all-gather.7.cloned.1.call-done = f32[768,512]{1,0:T(8,128)} async-done(((f32[768,128]{1,0:T(8,128)}), f32[768,512]{1,0:T(8,128)}) %all-gather.7.cloned.1.call-update) | async-done | bytes 1572880 | tf_op jit(solution)/shard_map/all_gather | solution.py:108
  43.4 52.2 %all-reduce.322.cloned.1.call-done = f32[768,768]{1,0:T(8,128)} async-done(((f32[768,768]{1,0:T(8,128)}), f32[768,768]{1,0:T(8,128)}) %all-reduce.322.cloned.1.call-update) | async-done | bytes 2359312 | tf_op jit(solution)/shard_map/psum | solution.py:125
  154.0 8.2 all_gather.25
  164.5 20.4 %all-gather.9.cloned.1.call-done = f32[768,512]{1,0:T(8,128)} async-done(((f32[768,128]{1,0:T(8,128)}), f32[768,512]{1,0:T(8,128)}) %all-gather.9.cloned.1.call-update) | async-done | bytes 1572880 | tf_op jit(solution)/shard_map/all_gather | solution.py:108
  192.1 55.7 %all-reduce.324.cloned.1.call-done = f32[768,768]{1,0:T(8,128)} async-done(((f32[768,768]{1,0:T(8,128)}), f32[768,768]{1,0:T(8,128)}) %all-reduce.324.cloned.1.call-update) | async-done | bytes 2359312 | tf_op jit(solution)/shard_map/psum | solution.py:125
  306.8 8.2 all_gather.27
  320.8 28.8 %reduce-scatter.3.cloned.1.call-done = f32[768,128]{1,0:T(8,128)} async-done(((f32[768,512]{1,0:T(8,128)}), f32[768,128]{1,0:T(8,128)}) %reduce-scatter.3.cloned.1.call-update) | async-done | bytes 393232 | tf_op jit(solution)/shard_map/reduce_scatter | solution.py:199
  357.1 93.9 %all-reduce.326.cloned.1.call-done = f32[768,1536]{1,0:T(8,128)} async-done(((f32[768,1536]{1,0:T(8,128)}), f32[768,1536]{1,0:T(8,128)}) %all-reduce.326.cloned.1.call-update) | async-done | bytes 4718608 | tf_op jit(solution)/shard_map/psum | solution.py:136
  451.0 5.1 fusion.478
  461.9 5.8 fusion.447
  494.6 4.0 fusion.445
  528.8 4.2 fusion.431
  586.3 4.0 fusion.441
  599.9 4.0 fusion.440
  659.7 19.4 %all-gather.13.cloned.1.call-done = f32[768,512]{1,0:T(8,128)} async-done(((f32[768,128]{1,0:T(8,128)}), f32[768,512]{1,0:T(8,128)}) %all-gather.13.cloned.1.call-update) | async-done | bytes 1572880 | tf_op jit(solution)/shard_map/all_gather | solution.py:118
  680.7 20.4 %all-gather.11.cloned.1.call-done = f32[768,512]{1,0:T(8,128)} async-done(((f32[768,128]{1,0:T(8,128)}), f32[768,512]{1,0:T(8,128)}) %all-gather.11.cloned.1.call-update) | async-done | bytes 1572880 | tf_op jit(solution)/shard_map/all_gather | solution.py:117
  707.7 28.3 %reduce-scatter.5.cloned.1.call-done = f32[768,128]{1,0:T(8,128)} async-done(((f32[768,512]{1,0:T(8,128)}), f32[768,128]{1,0:T(8,128)}) %reduce-scatter.5.cloned.1.call-update) | async-done | bytes 393232 | tf_op jit(solution)/shard_map/reduce_scatter | solution.py:199
  742.3 93.7 %all-reduce.328.cloned.1.call-done = f32[768,1536]{1,0:T(8,128)} async-done(((f32[768,1536]{1,0:T(8,128)}), f32[768,1536]{1,0:T(8,128)}) %all-reduce.328.cloned.1.call-update) | async-done | bytes 4718608 | tf_op jit(solution)/shard_map/psum | solution.py:136
  836.0 4.8 fusion.477
  846.5 5.0 fusion.423
  964.5 4.0 fusion.417
  978.2 4.0 fusion.416
  1049.8 37.1 %all-reduce.314 = (f32[2,4,128]{2,1,0:T(4,128)S(1)}, f32[2,3,384]{2,1,0:T(4,128)S(1)}) all-reduce(f32[2,4,128]{2,1,0:T(4,128)S(1)} %pad_maximum_fusion.10, f32[2,3,384]{2,1,0:T(4,128)S(1)} %pad_maximum_fusion.9), channel_id=1, replica_groups=mesh['seq'=8,'feat'=4] {'seq'}, use_global_device_ids=true, to_apply=%region_28.0 | all-reduce | flops 3328 | bytes 26624 | tf_op jit(solution)/shard_map/psum | solution.py:221
  1095.4 110.1 %all-reduce.330.cloned.1.call-done = (f32[2,128,768]{2,1,0:T(8,128)}, f32[2,1536,128]{2,1,0:T(8,128)}, f32[2,512,128]{2,1,0:T(8,128)}) async-done(((f32[2,128,768]{2,1,0:T(8,128)}, f32[2,1536,128]{2,1,0:T(8,128)}, f32[2,512,128]{2,1,0:T(8,128)}), (f32[2,128,768]{2,1,0:T(8,128)}, f32[2,1536,128]{2,1,0:T(8,128)}, f32[2,512,128]{2,1,0:T(8,128)})) %all-reduce.330.cloned.1.call-update) | async-done | bytes 2883600 | tf_op jit(solution)/shard_map/psum | solution.py:221
  (1637 shorter events, 558.3 us)
Async XLA Ops:
  7.2 25.5 %all-gather.7.cloned.1.call-start = ((), (), s32[]{:S(2)}) async-start(), calls=%async_computation.2 | async-start | bytes 1966080 | tf_op jit(solution)/shard_map/all_gather | solution.py:108
  9.0 86.5 %all-reduce.322.cloned.1.call-start = ((), (), s32[]{:S(2)}) async-start(), calls=%async_computation.3 | async-start | bytes 4718592 | tf_op jit(solution)/shard_map/psum | solution.py:125
  39.8 145.1 %all-gather.9.cloned.1.call-start = ((), (), s32[]{:S(2)}) async-start(), calls=%async_computation.4 | async-start | bytes 1966080 | tf_op jit(solution)/shard_map/all_gather | solution.py:108
  43.4 54.2 %copy-start.553 = (f32[384]{0:T(512)}, f32[384]{0:T(512)S(1)}, u32[]{:S(2)}) copy-start(f32[384]{0:T(512)S(1)} %get-tuple-element.706) | copy-start | bytes 4612
  43.4 54.2 %copy-start.555 = (f32[384]{0:T(512)}, f32[384]{0:T(512)S(1)}, u32[]{:S(2)}) copy-start(f32[384]{0:T(512)S(1)} %get-tuple-element.707) | copy-start | bytes 4612
  164.4 83.3 %all-reduce.324.cloned.1.call-start = ((), (), s32[]{:S(2)}) async-start(), calls=%async_computation.5 | async-start | bytes 4718592 | tf_op jit(solution)/shard_map/psum | solution.py:125
  192.0 157.6 %reduce-scatter.3.cloned.1.call-start = ((), (), s32[]{:S(2)}) async-start(), calls=%async_computation.6 | async-start | bytes 1966080 | tf_op jit(solution)/shard_map/reduce_scatter | solution.py:199
  192.1 57.7 %copy-start.557 = (f32[384]{0:T(512)}, f32[384]{0:T(512)S(1)}, u32[]{:S(2)}) copy-start(f32[384]{0:T(512)S(1)} %get-tuple-element.700) | copy-start | bytes 4612
  192.1 57.7 %copy-start.559 = (f32[384]{0:T(512)}, f32[384]{0:T(512)S(1)}, u32[]{:S(2)}) copy-start(f32[384]{0:T(512)S(1)} %get-tuple-element.701) | copy-start | bytes 4612
  320.8 130.2 %all-reduce.326.cloned.1.call-start = ((), (), s32[]{:S(2)}) async-start(), calls=%async_computation.7 | async-start | bytes 9437184 | tf_op jit(solution)/shard_map/psum | solution.py:136
  356.8 322.2 %all-gather.13.cloned.1.call-start = ((), (), s32[]{:S(2)}) async-start(), calls=%async_computation.9 | async-start | bytes 1966080 | tf_op jit(solution)/shard_map/all_gather | solution.py:118
  658.9 42.2 %all-gather.11.cloned.1.call-start = ((), (), s32[]{:S(2)}) async-start(), calls=%async_computation.8 | async-start | bytes 1966080 | tf_op jit(solution)/shard_map/all_gather | solution.py:117
  659.6 76.4 %reduce-scatter.5.cloned.1.call-start = ((), (), s32[]{:S(2)}) async-start(), calls=%async_computation.10 | async-start | bytes 1966080 | tf_op jit(solution)/shard_map/reduce_scatter | solution.py:199
  707.7 128.3 %all-reduce.328.cloned.1.call-start = ((), (), s32[]{:S(2)}) async-start(), calls=%async_computation.11 | async-start | bytes 9437184 | tf_op jit(solution)/shard_map/psum | solution.py:136
  741.8 94.2 %copy-start.450 = (f32[256,384]{1,0:T(8,128)S(1)}, f32[256,384]{1,0:T(8,128)}, u32[]{:S(2)}) copy-start(f32[256,384]{1,0:T(8,128)} %copy-done.449) | copy-start | bytes 1179652
  741.8 94.2 %copy-start.452 = (f32[256,384]{1,0:T(8,128)S(1)}, f32[256,384]{1,0:T(8,128)}, u32[]{:S(2)}) copy-start(f32[256,384]{1,0:T(8,128)} %copy-done.451) | copy-start | bytes 1179652
  741.8 348.1 %all-gather.17.cloned.1.call-start = ((), (), s32[]{:S(2)}) async-start(), calls=%async_computation.13 | async-start | bytes 1966080 | tf_op jit(solution)/shard_map/all_gather | solution.py:118
  1035.7 55.9 %all-gather.15.cloned.1.call-start = ((), (), s32[]{:S(2)}) async-start(), calls=%async_computation.12 | async-start | bytes 1966080 | tf_op jit(solution)/shard_map/all_gather | solution.py:117
  1036.3 169.1 %all-reduce.330.cloned.1.call-start = ((), (), s32[]{:S(2)}) async-start(), calls=%async_computation.14 | async-start | bytes 5767168 | tf_op jit(solution)/shard_map/psum | solution.py:221
  1048.5 40.8 %copy-start.562 = (f32[2,4,128]{2,1,0:T(4,128)S(1)}, f32[2,4,128]{2,1,0:T(4,128)}, u32[]{:S(2)}) copy-start(f32[2,4,128]{2,1,0:T(4,128)} %param.26) | copy-start | bytes 12292
  1048.5 40.8 %copy-start.577 = (f32[2,4,128]{2,1,0:T(4,128)S(1)}, f32[2,4,128]{2,1,0:T(4,128)}, u32[]{:S(2)}) copy-start(f32[2,4,128]{2,1,0:T(4,128)} %param.36) | copy-start | bytes 12292
  1091.6 113.9 %copy-start.515 = (f32[2,512,128]{2,1,0:T(8,128)S(1)}, f32[2,512,128]{2,1,0:T(8,128)}, u32[]{:S(2)}) copy-start(f32[2,512,128]{2,1,0:T(8,128)} %param.25) | copy-start | bytes 1572868
  1091.6 113.9 %copy-start.547 = (f32[2,512,128]{2,1,0:T(8,128)S(1)}, f32[2,512,128]{2,1,0:T(8,128)}, u32[]{:S(2)}) copy-start(f32[2,512,128]{2,1,0:T(8,128)} %param.35) | copy-start | bytes 1572868
  1091.6 113.9 %copy-start.548 = (f32[2,512,128]{2,1,0:T(8,128)S(1)}, f32[2,512,128]{2,1,0:T(8,128)}, u32[]{:S(2)}) copy-start(f32[2,512,128]{2,1,0:T(8,128)} %param.30) | copy-start | bytes 1572868
  (581 other events, 1808.2 us)
Sparse Core Ops, SparseCore 0:
  10.2 22.5 all-gather.6
  39.9 55.6 all-reduce.321
  164.6 20.2 all-gather.8
  192.1 55.6 all-reduce.323
  320.9 28.6 reduce-scatter.2
  356.9 94.0 all-reduce.325
  659.0 19.9 all-gather.12
  681.2 19.8 all-gather.10
  707.8 28.1 reduce-scatter.4
  742.0 94.0 all-reduce.327
  1035.9 19.9 all-gather.16
  1057.9 19.8 all-gather.14
  1082.3 123.1 all-reduce.329
where the time goes:
time: 1230 us; the launch traced here: 1220 us
  waiting for transfers between devices  546 us (44%)
  other arithmetic  391 us (32%)
  local copies, waits for them, and re-layouts  167 us (14%)
  blocking collectives  53.4 us (4%)
  matrix products  42.7 us (3%)
  between operations  20.4 us (2%)
    psum x2, waiting for transfers between devices, state_backward(): states_grad = lax.psum(partial_states, 'feat')  188 us
    unnamed x1188, local copies, waits for them, and re-layouts  153 us
    neg x32, other arithmetic, combine(): mult_real = later[0] * earlier[0] - later[1] * earlier[1]  115 us
    psum x1, waiting for transfers between devices, body(): lax.psum((stacked_in, stacked_out, stacked_gate, stacked_feature, stacked...  110 us
    psum x2, waiting for transfers between devices, state_forward(): drive = lax.psum(partial_drive, 'feat')  108 us
    add_any x40, other arithmetic, combine(): add_real = later[0] * earlier[2] - later[1] * earlier[3] + later[2]  59.8 us
    neg x36, other arithmetic, combine(): add_real = later[0] * earlier[2] - later[1] * earlier[3] + later[2]  58.3 us
    reduce_scatter x2, waiting for transfers between devices, body(): lax.psum_scatter(contract_cols(pre_grad, gate_low), 'feat', scatter_dimen...  57 us
  transfers between devices with their start and end apart: 13, of which 11 were waited for; matrix products, arithmetic and copies ran while one was open for 2% of the time, Pallas kernels for 0%

commit v1 on v0

--- a/solution.py
+++ b/solution.py
@@ -105,7 +105,12 @@
 
 
 def moments(stream):
-    whole = lax.all_gather(stream, "feat", axis=1, tiled=True)
+    ring = [stream]
+    for hop in range(3):
+        ring.append(lax.ppermute(ring[-1], "feat", [(dev, (dev + 1) % 4) for dev in range(4)]))
+    whole = jnp.roll(
+        jnp.concatenate(ring[::-1], axis=1), (lax.axis_index("feat") + 1) * ring[0].shape[1], axis=1
+    )
     center = jnp.mean(whole, 1, keepdims=True)
     spread = whole - center
     variance = jnp.mean(spread * spread, 1, keepdims=True)

time: 1230 us -> 1230 us (level)
    all_gather x2 -> x0, waiting for transfers between devices: 42.6 us -> none  [moments(): whole = lax.all_gather(stream, 'feat', axis=1, tiled=True)]
    ppermute x0 -> x6, waiting for transfers between devices: none -> 40.5 us  [moments(): lax.ppermute(ring[-1], 'feat', [(dev, (dev + 1) % 4) for dev in range(4)])]
    unnamed x1188 -> x1182, local copies, waits for them, and re-layouts: 153 us -> 153 us
  transfers between devices with their start and end apart: 13 -> 17, of which waited for: 11 -> 15; matrix products, arithmetic and copies ran while one was open for 2% -> 2% of each run, Pallas kernels for 0% -> 0%
where the time goes in v1:
time: 1230 us; the launch traced here: 1220 us
  waiting for transfers between devices  547 us (44%)
  other arithmetic  390 us (32%)
  local copies, waits for them, and re-layouts  167 us (14%)
  blocking collectives  53.4 us (4%)
  matrix products  42.6 us (3%)
  between operations  20.2 us (2%)
    psum x2, waiting for transfers between devices, state_backward(): states_grad = lax.psum(partial_states, 'feat')  188 us
    unnamed x1182, local copies, waits for them, and re-layouts  153 us
    neg x32, other arithmetic, combine(): mult_real = later[0] * earlier[0] - later[1] * earlier[1]  115 us
    psum x2, waiting for transfers between devices, state_forward(): drive = lax.psum(partial_drive, 'feat')  110 us
    psum x1, waiting for transfers between devices, body(): lax.psum((stacked_in, stacked_out, stacked_gate, stacked_feature, stacked...  110 us
    add_any x40, other arithmetic, combine(): add_real = later[0] * earlier[2] - later[1] * earlier[3] + later[2]  59.9 us
    neg x36, other arithmetic, combine(): add_real = later[0] * earlier[2] - later[1] * earlier[3] + later[2]  58.3 us
    reduce_scatter x2, waiting for transfers between devices, body(): lax.psum_scatter(contract_cols(pre_grad, gate_low), 'feat', scatter_dimen...  57 us
  transfers between devices with their start and end apart: 17, of which 15 were waited for; matrix products, arithmetic and copies ran while one was open for 2% of the time, Pallas kernels for 0%

profile of v1, /device:TPU:0, one launch (start us, length us, event | category | flops | bytes accessed | tf_op | source)
XLA Modules:
  0.0 1221.5 jit_solution(9681904636097805894)
XLA Ops:
  8.7 7.4 collective-permute-done
  16.1 7.2 collective-permute-done.1
  25.8 4.7 collective-permute-done.2
  40.4 54.2 %all-reduce.322.cloned.1.call-done = f32[768,768]{1,0:T(8,128)} async-done(((f32[768,768]{1,0:T(8,128)}), f32[768,768]{1,0:T(8,128)}) %all-reduce.322.cloned.1.call-update) | async-done | bytes 2359312 | tf_op jit(solution)/shard_map/psum | solution.py:130
  153.0 8.2 all_gather.18
  163.8 6.8 collective-permute-done.3
  170.6 7.2 collective-permute-done.4
  177.8 7.2 collective-permute-done.5
  191.5 56.1 %all-reduce.324.cloned.1.call-done = f32[768,768]{1,0:T(8,128)} async-done(((f32[768,768]{1,0:T(8,128)}), f32[768,768]{1,0:T(8,128)}) %all-reduce.324.cloned.1.call-update) | async-done | bytes 2359312 | tf_op jit(solution)/shard_map/psum | solution.py:130
  306.2 8.2 all_gather.19
  320.3 28.8 %reduce-scatter.3.cloned.1.call-done = f32[768,128]{1,0:T(8,128)} async-done(((f32[768,512]{1,0:T(8,128)}), f32[768,128]{1,0:T(8,128)}) %reduce-scatter.3.cloned.1.call-update) | async-done | bytes 393232 | tf_op jit(solution)/shard_map/reduce_scatter | solution.py:204
  356.7 93.7 %all-reduce.326.cloned.1.call-done = f32[768,1536]{1,0:T(8,128)} async-done(((f32[768,1536]{1,0:T(8,128)}), f32[768,1536]{1,0:T(8,128)}) %all-reduce.326.cloned.1.call-update) | async-done | bytes 4718608 | tf_op jit(solution)/shard_map/psum | solution.py:141
  450.4 5.1 fusion.496
  461.3 5.8 fusion.461
  599.1 4.0 fusion.454
  658.9 19.5 %all-gather.7.cloned.1.call-done = f32[768,512]{1,0:T(8,128)} async-done(((f32[768,128]{1,0:T(8,128)}), f32[768,512]{1,0:T(8,128)}) %all-gather.7.cloned.1.call-update) | async-done | bytes 1572880 | tf_op jit(solution)/shard_map/all_gather | solution.py:123
  680.1 20.2 %all-gather.5.cloned.1.call-done = f32[768,512]{1,0:T(8,128)} async-done(((f32[768,128]{1,0:T(8,128)}), f32[768,512]{1,0:T(8,128)}) %all-gather.5.cloned.1.call-update) | async-done | bytes 1572880 | tf_op jit(solution)/shard_map/all_gather | solution.py:122
  707.0 28.3 %reduce-scatter.5.cloned.1.call-done = f32[768,128]{1,0:T(8,128)} async-done(((f32[768,512]{1,0:T(8,128)}), f32[768,128]{1,0:T(8,128)}) %reduce-scatter.5.cloned.1.call-update) | async-done | bytes 393232 | tf_op jit(solution)/shard_map/reduce_scatter | solution.py:204
  741.3 93.9 %all-reduce.328.cloned.1.call-done = f32[768,1536]{1,0:T(8,128)} async-done(((f32[768,1536]{1,0:T(8,128)}), f32[768,1536]{1,0:T(8,128)}) %all-reduce.328.cloned.1.call-update) | async-done | bytes 4718608 | tf_op jit(solution)/shard_map/psum | solution.py:141
  835.3 4.8 fusion.495
  845.8 5.0 fusion.437
  904.1 4.1 fusion.421
  1049.3 37.1 %all-reduce.314 = (f32[2,4,128]{2,1,0:T(4,128)S(1)}, f32[2,3,384]{2,1,0:T(4,128)S(1)}) all-reduce(f32[2,4,128]{2,1,0:T(4,128)S(1)} %pad_maximum_fusion.10, f32[2,3,384]{2,1,0:T(4,128)S(1)} %pad_maximum_fusion.9), channel_id=1, replica_groups=mesh['seq'=8,'feat'=4] {'seq'}, use_global_device_ids=true, to_apply=%region_28.30 | all-reduce | flops 3328 | bytes 26624 | tf_op jit(solution)/shard_map/psum | solution.py:226
  1094.8 110.2 %all-reduce.330.cloned.1.call-done = (f32[2,128,768]{2,1,0:T(8,128)}, f32[2,1536,128]{2,1,0:T(8,128)}, f32[2,512,128]{2,1,0:T(8,128)}) async-done(((f32[2,128,768]{2,1,0:T(8,128)}, f32[2,1536,128]{2,1,0:T(8,128)}, f32[2,512,128]{2,1,0:T(8,128)}), (f32[2,128,768]{2,1,0:T(8,128)}, f32[2,1536,128]{2,1,0:T(8,128)}, f32[2,512,128]{2,1,0:T(8,128)})) %all-reduce.330.cloned.1.call-update) | async-done | bytes 2883600 | tf_op jit(solution)/shard_map/psum | solution.py:226
  (1637 shorter events, 573.5 us)
Async XLA Ops:
  7.2 87.5 %all-reduce.322.cloned.1.call-start = ((), (), s32[]{:S(2)}) async-start(), calls=%async_computation.2 | async-start | bytes 4718592 | tf_op jit(solution)/shard_map/psum | solution.py:130
  8.2 7.9 collective-permute-start
  16.1 7.2 collective-permute-start.1
  23.3 7.2 collective-permute-start.2
  36.8 210.8 %all-reduce.324.cloned.1.call-start = ((), (), s32[]{:S(2)}) async-start(), calls=%async_computation.3 | async-start | bytes 4718592 | tf_op jit(solution)/shard_map/psum | solution.py:130
  163.4 7.3 collective-permute-start.3
  170.6 7.2 collective-permute-start.4
  177.8 7.2 collective-permute-start.5
  191.4 157.7 %reduce-scatter.3.cloned.1.call-start = ((), (), s32[]{:S(2)}) async-start(), calls=%async_computation.4 | async-start | bytes 1966080 | tf_op jit(solution)/shard_map/reduce_scatter | solution.py:204
  191.5 58.1 %copy-start.554 = (f32[384]{0:T(512)}, f32[384]{0:T(512)S(1)}, u32[]{:S(2)}) copy-start(f32[384]{0:T(512)S(1)} %get-tuple-element.705) | copy-start | bytes 4612
  191.5 58.1 %copy-start.556 = (f32[384]{0:T(512)}, f32[384]{0:T(512)S(1)}, u32[]{:S(2)}) copy-start(f32[384]{0:T(512)S(1)} %get-tuple-element.706) | copy-start | bytes 4612
  320.2 130.2 %all-reduce.326.cloned.1.call-start = ((), (), s32[]{:S(2)}) async-start(), calls=%async_computation.5 | async-start | bytes 9437184 | tf_op jit(solution)/shard_map/psum | solution.py:141
  356.3 322.1 %all-gather.7.cloned.1.call-start = ((), (), s32[]{:S(2)}) async-start(), calls=%async_computation.7 | async-start | bytes 1966080 | tf_op jit(solution)/shard_map/all_gather | solution.py:123
  658.2 42.1 %all-gather.5.cloned.1.call-start = ((), (), s32[]{:S(2)}) async-start(), calls=%async_computation.6 | async-start | bytes 1966080 | tf_op jit(solution)/shard_map/all_gather | solution.py:122
  658.8 76.5 %reduce-scatter.5.cloned.1.call-start = ((), (), s32[]{:S(2)}) async-start(), calls=%async_computation.8 | async-start | bytes 1966080 | tf_op jit(solution)/shard_map/reduce_scatter | solution.py:204
  707.0 128.3 %all-reduce.328.cloned.1.call-start = ((), (), s32[]{:S(2)}) async-start(), calls=%async_computation.9 | async-start | bytes 9437184 | tf_op jit(solution)/shard_map/psum | solution.py:141
  741.1 94.2 %copy-start.450 = (f32[256,384]{1,0:T(8,128)S(1)}, f32[256,384]{1,0:T(8,128)}, u32[]{:S(2)}) copy-start(f32[256,384]{1,0:T(8,128)} %copy-done.449) | copy-start | bytes 1179652
  741.1 94.2 %copy-start.452 = (f32[256,384]{1,0:T(8,128)S(1)}, f32[256,384]{1,0:T(8,128)}, u32[]{:S(2)}) copy-start(f32[256,384]{1,0:T(8,128)} %copy-done.451) | copy-start | bytes 1179652
  741.1 348.3 %all-gather.11.cloned.1.call-start = ((), (), s32[]{:S(2)}) async-start(), calls=%async_computation.11 | async-start | bytes 1966080 | tf_op jit(solution)/shard_map/all_gather | solution.py:123
  1035.2 55.9 %all-gather.9.cloned.1.call-start = ((), (), s32[]{:S(2)}) async-start(), calls=%async_computation.10 | async-start | bytes 1966080 | tf_op jit(solution)/shard_map/all_gather | solution.py:122
  1035.8 169.1 %all-reduce.330.cloned.1.call-start = ((), (), s32[]{:S(2)}) async-start(), calls=%async_computation.12 | async-start | bytes 5767168 | tf_op jit(solution)/shard_map/psum | solution.py:226
  1091.0 113.9 %copy-start.512 = (f32[2,512,128]{2,1,0:T(8,128)S(1)}, f32[2,512,128]{2,1,0:T(8,128)}, u32[]{:S(2)}) copy-start(f32[2,512,128]{2,1,0:T(8,128)} %param.27) | copy-start | bytes 1572868
  1091.1 113.9 %copy-start.544 = (f32[2,512,128]{2,1,0:T(8,128)S(1)}, f32[2,512,128]{2,1,0:T(8,128)}, u32[]{:S(2)}) copy-start(f32[2,512,128]{2,1,0:T(8,128)} %param.37) | copy-start | bytes 1572868
  1091.1 113.9 %copy-start.545 = (f32[2,512,128]{2,1,0:T(8,128)S(1)}, f32[2,512,128]{2,1,0:T(8,128)}, u32[]{:S(2)}) copy-start(f32[2,512,128]{2,1,0:T(8,128)} %param.32) | copy-start | bytes 1572868
  (582 other events, 2031.2 us)
Sparse Core Ops, SparseCore 0:
  36.9 57.6 all-reduce.321
  191.5 56.0 all-reduce.323
  320.3 28.6 reduce-scatter.2
  356.4 94.0 all-reduce.325
  658.4 19.9 all-gather.6
  680.5 19.8 all-gather.4
  707.1 28.1 reduce-scatter.4
  741.2 94.0 all-reduce.327
  1035.4 19.9 all-gather.10
  1057.4 19.8 all-gather.8
  1081.8 123.1 all-reduce.329
